TPU v7x, 32 devices: a whole 2x2x4 slice. The times are simulated.
32 devices in a mesh: dp: 8 (over z, core), tensor: 4 (over y, x).
Axes of the slice: x: 2, y: 2, z: 4, core: 2. Of those that a mesh axis runs over, the one named last changes fastest.
Arguments:
- tokens: bfloat16 [4096, 4096], P('dp', 'tensor'), may hold values from -6 to 6
- butterfly: bfloat16 [64, 5, 256, 256], P('tensor', None, 'dp'), may hold values from -0.15625 to 0.15625
- left_factor: bfloat16 [4096, 256], P(('tensor', 'dp')), may hold values from -0.09375 to 0.09375
- right_factor: bfloat16 [256, 16384], P('dp', 'tensor'), may hold values from -0.375 to 0.375
- cotangent: bfloat16 [4096, 16384], P('dp', 'tensor'), may hold values from -6 to 6
Outputs:
- hidden: bfloat16 [4096, 16384], P('dp', 'tensor')
- grad_tokens: bfloat16 [4096, 4096], P('dp', 'tensor')
- grad_butterfly: bfloat16 [64, 5, 256, 256], P('tensor', None, 'dp')
- grad_left: bfloat16 [4096, 256], P(('tensor', 'dp'))
- grad_right: bfloat16 [256, 16384], P('dp', 'tensor')
All inputs are finite; a program needn't handle non-finite values.
Results may differ from a plain program's by a relative error of at most 0.02.
Values may be sent and summed in bfloat16 or wider, within the bound.
A program may use at most 128 MiB of HBM per device.

v0:
```python
import jax
import jax.numpy as jnp
from jax import lax
from jax.sharding import PartitionSpec as P

BLK = 256
LOG = 4
ROOT_HALF = 0.7071067811865476
INV_ROOT_TWO_PI = 0.3989422804014327


def swapped(block, axis, stride):
    count = lax.axis_size(axis)
    route = []
    for low in range(count):
        high = low | 1 << stride
        if high != low and high < count:
            route += [(low, high), (high, low)]
    return lax.ppermute(block, axis, route)


def gelu_pair(preact):
    cdf = 0.5 * (1.0 + jax.scipy.special.erf(preact * ROOT_HALF))
    return (preact * cdf, cdf + preact * INV_ROOT_TWO_PI * jnp.exp(-0.5 * preact * preact))


def flip_blocks(blocks, stride):
    full_shape = blocks.shape
    leading = full_shape[:-2]
    block_count = full_shape[-2]
    halves = blocks.reshape(leading + (block_count // (2 * stride), 2, stride, full_shape[-1]))
    return jnp.flip(halves, axis=-3).reshape(full_shape)


def per_device(tokens, butterfly, left_factor, right_factor, cotangent):
    rows_here = tokens.shape[0]
    blocks_here = tokens.shape[1] // BLK
    shift_bits = blocks_here.bit_length() - 1
    hidden_blocks = right_factor.shape[1] // BLK
    group_ratio = hidden_blocks // blocks_here
    weights, left_full, right_full = (
        lax.all_gather(butterfly, "dp", axis=2, tiled=True),
        lax.all_gather(left_factor, "dp", axis=0, tiled=True),
        lax.all_gather(right_factor, "dp", axis=0, tiled=True),
    )
    blocks = tokens.reshape(rows_here, blocks_here, BLK)
    partners = [blocks]
    for level in range(LOG):
        if 1 << level < blocks_here:
            partners.append(flip_blocks(blocks, 1 << level))
        else:
            partners.append(swapped(blocks, "tensor", level - shift_bits))
    stacked = jnp.stack(partners)
    weight_blocks = weights.reshape(blocks_here, group_ratio, LOG + 1, BLK, BLK)
    preact = jnp.einsum(
        "ktqi,qrkio->tqro", stacked, weight_blocks, preferred_element_type=jnp.float32
    )
    preact = preact.reshape(rows_here, hidden_blocks * BLK)
    low_part = jnp.dot(tokens, left_full, preferred_element_type=jnp.float32)
    low_rank = lax.psum(low_part.astype(jnp.bfloat16), "tensor")
    preact = preact + jnp.dot(low_rank, right_full, preferred_element_type=jnp.float32)
    activation, slopes = gelu_pair(preact)
    hidden = activation.astype(jnp.bfloat16)
    grad_pre = (cotangent.astype(jnp.float32) * slopes).astype(jnp.bfloat16)
    grad_wide = grad_pre.reshape(rows_here, blocks_here, group_ratio, BLK)
    grad_weight = jnp.einsum(
        "ktqi,tqro->qrkio", stacked, grad_wide, preferred_element_type=jnp.float32
    )
    grad_weight = grad_weight.reshape(hidden_blocks, LOG + 1, BLK, BLK)
    low_back = jnp.einsum("th,rh->tr", grad_pre, right_full, preferred_element_type=jnp.float32)
    grad_low = lax.psum(low_back.astype(jnp.bfloat16), "tensor")
    grad_first = jnp.einsum("td,tr->dr", tokens, grad_low, preferred_element_type=jnp.float32)
    grad_second = jnp.einsum("tr,th->rh", low_rank, grad_pre, preferred_element_type=jnp.float32)
    returned = jnp.einsum(
        "tqro,qrkio->ktqi", grad_wide, weight_blocks, preferred_element_type=jnp.float32
    )
    summed = returned[0]
    for level in range(LOG):
        contrib = returned[level + 1]
        if 1 << level < blocks_here:
            summed = summed + flip_blocks(contrib, 1 << level)
        else:
            summed = summed + swapped(
                contrib.astype(jnp.bfloat16), "tensor", level - shift_bits
            ).astype(contrib.dtype)
    grad_input = summed.reshape(rows_here, blocks_here * BLK)
    grad_input = grad_input + jnp.einsum(
        "tr,dr->td", grad_low, left_full, preferred_element_type=jnp.float32
    )
    sum_weight, sum_first, sum_second = (
        lax.psum_scatter(
            grad_weight.astype(jnp.bfloat16), "dp", scatter_dimension=2, tiled=True
        ).astype(jnp.float32),
        lax.psum_scatter(
            grad_first.astype(jnp.bfloat16), "dp", scatter_dimension=0, tiled=True
        ).astype(jnp.float32),
        lax.psum_scatter(
            grad_second.astype(jnp.bfloat16), "dp", scatter_dimension=0, tiled=True
        ).astype(jnp.float32),
    )
    return (
        hidden,
        grad_input.astype(jnp.bfloat16),
        sum_weight.astype(jnp.bfloat16),
        sum_first.astype(jnp.bfloat16),
        sum_second.astype(jnp.bfloat16),
    )


def solution(mesh):
    placed = (
        P("dp", "tensor"),
        P("tensor", None, "dp", None),
        P(("tensor", "dp"), None),
        P("dp", "tensor"),
        P("dp", "tensor"),
    )
    return jax.shard_map(
        per_device,
        mesh=mesh,
        in_specs=placed,
        out_specs=(
            P("dp", "tensor"),
            P("dp", "tensor"),
            P("tensor", None, "dp", None),
            P(("tensor", "dp"), None),
            P("dp", "tensor"),
        ),
        check_vma=False,
    )
```

profile of v0, /device:TPU:0, one launch (start us, length us, event | category | flops | bytes accessed | tf_op | source)
XLA Modules:
  0.0 386.7 jit_solution(5141714083734337590)
XLA Ops:
  8.8 16.8 %all_gather.10 = bf16[1024,256]{1,0:T(8,128)(2,1)S(1)} all-gather(bf16[128,256]{1,0:T(8,128)(2,1)} %param.7), channel_id=1, replica_groups=mesh['dp'=8,'tensor'=4] {'dp'}, dimensions={0}, use_global_device_ids=true | all-gather | bytes 589824 | tf_op jit(solution)/shard_map/all_gather | solution.py:43
  26.4 2.4 convolution_convert_fusion.4
  39.1 2.3 copy.42
  42.8 2.4 copy.41
  45.2 2.3 rev.16
  48.5 2.3 constant_dynamic-update-slice_fusion.1
  51.8 8.5 %collective-permute-done = bf16[512,4,256]{2,0,1:T(8,128)(2,1)} collective-permute-done((bf16[512,4,256]{2,0,1:T(8,128)(2,1)}, bf16[512,4,256]{2,0,1:T(8,128)(2,1)}, u32[]{:S(2)}, u32[]{:S(2)}) %collective-permute-start) | collective-permute-done | bytes 1048608 | tf_op jit(solution)/shard_map/ppermute | solution.py:19
  60.3 2.3 bitcast_dynamic-update-slice_fusion.1
  62.6 2.3 bitcast_dynamic-update-slice_fusion
  64.8 47.8 %all-gather.3.cloned.1.call-done = bf16[16,5,256,256]{3,2,1,0:T(8,128)(2,1)} async-done(((bf16[16,5,32,256]{3,2,1,0:T(8,128)(2,1)}), bf16[16,5,256,256]{3,2,1,0:T(8,128)(2,1)}) %all-gather.3.cloned.1.call-update) | async-done | bytes 10485776 | tf_op jit(solution)/shard_map/all_gather | solution.py:42
  112.6 11.9 %fusion.6 = f32[4,512,4,256,1]{1,3,4,2,0:T(8,128)} fusion(bf16[4,4,5,256,256]{4,3,2,1,0:T(8,128)(2,1)} %bitcast.93, bf16[5,512,4,256]{3,1,0,2:T(8,128)(2,1)} %bitcast_dynamic-update-slice_fusion), kind=kOutput, calls=%fused_computation.11 | convolution fusion | flops 5368709120 | bytes 24117248 | tf_op jit(solution)/shard_map/ktqi,qrkio->tqro/dot_general | solution.py:55
  124.5 9.0 %copy.48 = f32[512,4096]{1,0:T(8,128)} copy(f32[512,4096]{0,1:T(8,128)} %bitcast.88) | data formatting | bytes 16777216 | tf_op jit(solution)/shard_map/reshape | solution.py:58
  133.5 8.6 %all-gather.5.cloned.1.call-done = bf16[256,4096]{1,0:T(8,128)(2,1)} async-done(((bf16[32,4096]{1,0:T(8,128)(2,1)}), bf16[256,4096]{1,0:T(8,128)(2,1)}) %all-gather.5.cloned.1.call-update) | async-done | bytes 2097168 | tf_op jit(solution)/shard_map/all_gather | solution.py:44
  142.1 10.0 %fusion.4 = (bf16[512,4096]{1,0:T(8,128)(2,1)S(1)}, bf16[512,4096]{1,0:T(8,128)(2,1)}) fusion(bf16[512,4096]{1,0:T(8,128)(2,1)} %param.9, f32[512,4096]{1,0:T(8,128)} %copy.48, bf16[512,256]{1,0:T(8,128)(2,1)} %all-reduce.3.cloned.1.call-done, bf16[256,4096]{1,0:T(8,128)(2,1)} %all-gather.5.cloned.1.call-done), kind=kOutput, calls=%fused_computation.5 | convolution fusion | flops 1103101952 | bytes 23330816 | tf_op jit(solution)/shard_map/dot_general | solution.py:61
  152.1 2.1 copy-done.1
  154.2 2.0 convolution_convert_fusion.3
  156.3 42.0 %all-reduce.5.cloned.1.call-done = bf16[512,256]{1,0:T(8,128)(2,1)} async-done(((bf16[512,256]{1,0:T(8,128)(2,1)}), bf16[512,256]{1,0:T(8,128)(2,1)}) %all-reduce.5.cloned.1.call-update) | async-done | bytes 262160 | tf_op jit(solution)/shard_map/psum | solution.py:71
  200.9 4.8 %convolution_convert_fusion.1 = bf16[256,4096]{1,0:T(8,128)(2,1)} fusion(bf16[512,256]{1,0:T(8,128)(2,1)S(1)} %copy-done.6, bf16[512,4096]{1,0:T(8,128)(2,1)} %copy-done.1), kind=kOutput, calls=%fused_computation.13 | convolution fusion | flops 1074790400 | bytes 6553600 | tf_op jit(solution)/shard_map/tr,th->rh/dot_general | solution.py:73
  205.8 7.9 %reshape.38 = bf16[512,4,4,256]{3,2,1,0:T(4,128)(2,1)} reshape(bf16[512,4096]{1,0:T(8,128)(2,1)} %copy-done.1) | data formatting | bytes 8388608 | tf_op jit(solution)/shard_map/reshape | solution.py:65
  213.7 7.5 %copy.62 = bf16[512,4,4,256,1]{0,3,4,2,1:T(8,128)(2,1)} copy(bf16[512,4,4,256,1]{3,2,1,0,4:T(4,128)(2,1)} %bitcast.83) | data formatting | bytes 8388608 | tf_op jit(solution)/shard_map/reshape | solution.py:65
  221.2 11.3 %convolution_convert_fusion = bf16[4,4,256,5,256]{4,2,3,1,0:T(8,128)(2,1)} fusion(bf16[512,4,4,256,1]{0,3,4,2,1:T(8,128)(2,1)} %copy.62, bf16[5,512,4,256]{3,1,0,2:T(8,128)(2,1)} %bitcast_dynamic-update-slice_fusion), kind=kOutput, calls=%fused_computation.9 | convolution fusion | flops 5373952000 | bytes 19922944 | tf_op jit(solution)/shard_map/ktqi,tqro->qrkio/dot_general | solution.py:66
  232.4 15.2 %copy.55 = bf16[16,5,256,256]{3,2,1,0:T(8,128)(2,1)} copy(bf16[16,5,256,256]{2,3,1,0:T(8,128)(2,1)} %bitcast.84) | data formatting | bytes 20971520 | tf_op jit(solution)/shard_map/convert_element_type | solution.py:92
  247.6 12.8 %fusion.14 = (bf16[5,512,4,256]{1,3,0,2:T(8,128)(2,1)}, f32[5,512,4,256]{1,3,0,2:T(8,128)}) fusion(bf16[512,4,4,256,1]{0,3,4,2,1:T(8,128)(2,1)} %copy.62, bf16[4,4,5,256,256]{4,3,2,1,0:T(8,128)(2,1)} %bitcast.94), kind=kOutput, calls=%fused_computation.33 | convolution fusion | flops 5371330560 | bytes 30408704 | tf_op jit(solution)/shard_map/tqro,qrkio->ktqi/dot_general | solution.py:74
  260.4 3.1 slice_bitcast_fusion.2
  265.6 4.7 %fusion.13 = (f32[1,512,4,256]{1,3,0,2:T(8,128)}, f32[1,512,4,256]{1,3,0,2:T(8,128)}) fusion(f32[5,512,4,256]{1,3,0,2:T(8,128)} %get-tuple-element.27), kind=kLoop, calls=%fused_computation.32 | loop fusion | bytes 8388608 | tf_op jit(solution)/shard_map/slice | solution.py:79
  270.2 1.8 rev.18
  272.0 3.1 rev.19
  276.9 11.3 %collective-permute-done.2 = bf16[512,4,256]{0,2,1:T(8,128)(2,1)} collective-permute-done((bf16[512,4,256]{0,2,1:T(8,128)(2,1)}, bf16[512,4,256]{0,2,1:T(8,128)(2,1)}, u32[]{:S(2)}, u32[]{:S(2)}) %collective-permute-start.2) | collective-permute-done | bytes 1048608 | tf_op jit(solution)/shard_map/ppermute | solution.py:19
  289.6 5.0 %fusion.11 = f32[512,4,256]{0,2,1:T(8,128)} fusion(f32[5,512,4,256]{1,3,0,2:T(8,128)} %get-tuple-element.27, f32[512,1,2,2,256]{0,4,3,2,1:T(8,128)} %rev.19, f32[512,2,2,1,256]{0,4,2,1,3:T(8,128)S(1)} %rev.18, bf16[512,4,256]{0,2,1:T(8,128)(2,1)} %collective-permute-done.3, bf16[512,4,256]{0,2,1:T(8,128)(2,1)} %collective-permute-done.2), kind=kLoop, calls=%fused_computation.19 | loop fusion | flops 3145728 | bytes 10485760 | tf_op jit(solution)/shard_map/add | solution.py:83
  294.6 3.1 copy.53
  297.7 2.9 add_convert_fusion
  300.6 79.1 %reduce-scatter.6.cloned.1.call-done = bf16[16,5,32,256]{3,2,1,0:T(8,128)(2,1)} async-done(((bf16[16,5,256,256]{3,2,1,0:T(8,128)(2,1)}), bf16[16,5,32,256]{3,2,1,0:T(8,128)(2,1)}) %reduce-scatter.6.cloned.1.call-update) | async-done | bytes 1310736 | tf_op jit(solution)/shard_map/reduce_scatter | solution.py:91
  (49 shorter events, 23.3 us)
Async XLA Ops:
  8.0 27.5 %copy-start = (bf16[512,1024]{1,0:T(8,128)(2,1)S(1)}, bf16[512,1024]{1,0:T(8,128)(2,1)}, u32[]{:S(2)}) copy-start(bf16[512,1024]{1,0:T(8,128)(2,1)} %param.5) | copy-start | bytes 3145732
  8.0 104.6 %all-gather.3.cloned.1.call-start = ((), (), s32[]{:S(2)}) async-start(), calls=%async_computation.3 | async-start | bytes 11796480 | tf_op jit(solution)/shard_map/all_gather | solution.py:42
  8.7 124.8 %all-reduce.3.cloned.1.call-start = ((), (), s32[]{:S(2)}) async-start(), calls=%async_computation.4 | async-start | bytes 524288 | tf_op jit(solution)/shard_map/psum | solution.py:60
  25.6 0.8 copy-start.3
  28.8 113.3 %all-gather.5.cloned.1.call-start = ((), (), s32[]{:S(2)}) async-start(), calls=%async_computation.5 | async-start | bytes 2359296 | tf_op jit(solution)/shard_map/all_gather | solution.py:44
  29.6 168.7 %all-reduce.5.cloned.1.call-start = ((), (), s32[]{:S(2)}) async-start(), calls=%async_computation.6 | async-start | bytes 524288 | tf_op jit(solution)/shard_map/psum | solution.py:71
  32.5 27.8 %collective-permute-start = (bf16[512,4,256]{2,0,1:T(8,128)(2,1)}, bf16[512,4,256]{2,0,1:T(8,128)(2,1)}, u32[]{:S(2)}, u32[]{:S(2)}) collective-permute-start(bf16[512,4,256]{2,0,1:T(8,128)(2,1)} %copy.44), channel_id=1, source_target_pairs={{0,1},{1,0},{2,3},{3,2},{4,5},{5,4},{6,7},{7,6},{8,9},{9,8},{10,11... | collective-permute-start | bytes 3145736 | tf_op jit(solution)/shard_map/ppermute | solution.py:19
  34.0 28.6 %collective-permute-start.1 = (bf16[512,4,256]{2,0,1:T(8,128)(2,1)}, bf16[512,4,256]{2,0,1:T(8,128)(2,1)}, u32[]{:S(2)}, u32[]{:S(2)}) collective-permute-start(bf16[512,4,256]{2,0,1:T(8,128)(2,1)} %copy.44), channel_id=1, source_target_pairs={{0,2},{2,0},{1,3},{3,1},{4,6},{6,4},{5,7},{7,5},{8,10},{10,8},{9,1... | collective-permute-start | bytes 3145736 | tf_op jit(solution)/shard_map/ppermute | solution.py:19
  142.1 12.1 %copy-start.7 = (bf16[256,4096]{1,0:T(8,128)(2,1)S(1)}, bf16[256,4096]{1,0:T(8,128)(2,1)}, u32[]{:S(2)}) copy-start(bf16[256,4096]{1,0:T(8,128)(2,1)} %all-gather.5.cloned.1.call-done) | copy-start | bytes 6291460
  152.1 2.1 copy-start.1
  154.2 46.7 %copy-start.6 = (bf16[512,256]{1,0:T(8,128)(2,1)S(1)}, bf16[512,256]{1,0:T(8,128)(2,1)}, u32[]{:S(2)}) copy-start(bf16[512,256]{1,0:T(8,128)(2,1)} %all-reduce.3.cloned.1.call-done) | copy-start | bytes 786436
  156.2 144.3 %reduce-scatter.10.cloned.1.call-start = ((), (), s32[]{:S(2)}) async-start(), calls=%async_computation.9 | async-start | bytes 589824
  200.7 99.9 %reduce-scatter.8.cloned.1.call-start = ((), (), s32[]{:S(2)}) async-start(), calls=%async_computation.8 | async-start | bytes 2359296 | tf_op jit(solution)/shard_map/reduce_scatter | solution.py:97
  205.8 173.8 %reduce-scatter.6.cloned.1.call-start = ((), (), s32[]{:S(2)}) async-start(), calls=%async_computation.7 | async-start | bytes 11796480 | tf_op jit(solution)/shard_map/reduce_scatter | solution.py:91
  263.5 24.7 %collective-permute-start.2 = (bf16[512,4,256]{0,2,1:T(8,128)(2,1)}, bf16[512,4,256]{0,2,1:T(8,128)(2,1)}, u32[]{:S(2)}, u32[]{:S(2)}) collective-permute-start(bf16[512,4,256]{0,2,1:T(8,128)(2,1)} %get-tuple-element.24), channel_id=1, source_target_pairs={{0,1},{1,0},{2,3},{3,2},{4,5},{5,4},{6,7},{7,6},{8,9},{9,8},{10,11... | collective-permute-start | bytes 3145736 | tf_op jit(solution)/shard_map/ppermute | solution.py:19
  265.0 24.6 %collective-permute-start.3 = (bf16[512,4,256]{0,2,1:T(8,128)(2,1)}, bf16[512,4,256]{0,2,1:T(8,128)(2,1)}, u32[]{:S(2)}, u32[]{:S(2)}) collective-permute-start(bf16[512,4,256]{0,2,1:T(8,128)(2,1)} %get-tuple-element.25), channel_id=1, source_target_pairs={{0,2},{2,0},{1,3},{3,1},{4,6},{6,4},{5,7},{7,5},{8,10},{10,8},{9,1... | collective-permute-start | bytes 3145736 | tf_op jit(solution)/shard_map/ppermute | solution.py:19
  270.2 4.9 %copy-start.4 = (bf16[1024,256]{1,0:T(8,128)(2,1)S(1)}, bf16[1024,256]{1,0:T(8,128)(2,1)}, u32[]{:S(2)}) copy-start(bf16[1024,256]{1,0:T(8,128)(2,1)} %copy-done.3) | copy-start | bytes 1572868
  270.2 4.9 %copy-start.5 = (bf16[512,256]{1,0:T(8,128)(2,1)S(1)}, bf16[512,256]{1,0:T(8,128)(2,1)}, u32[]{:S(2)}) copy-start(bf16[512,256]{1,0:T(8,128)(2,1)} %all-reduce.5.cloned.1.call-done) | copy-start | bytes 786436
  294.6 3.1 copy-start.2
Sparse Core Ops, SparseCore 0:
  10.4 102.0 all-gather.2
  114.3 27.8 all-gather.4
  200.8 30.9 reduce-scatter.9
  234.6 33.9 reduce-scatter.7
  271.5 108.0 reduce-scatter.5
Sparse Core Ops, SparseCore 1:
  28.9 46.1 all-reduce.2
  156.3 41.9 all-reduce.4
where the time goes:
time: 388 us; the launch traced here: 387 us
  waiting for transfers between devices  200 us (52%)
  local copies, waits for them, and re-layouts  82.8 us (21%)
  matrix products  58.3 us (15%)
  blocking collectives  16.8 us (4%)
  between operations  15.3 us (4%)
  other arithmetic  7.92 us (2%)
  starting transfers between devices  5.51 us (1%)
    reduce_scatter x1, waiting for transfers between devices, per_device(): lax.psum_scatter(grad_weight.astype(jnp.bfloat16), 'dp', scatter_dimensio...  79.1 us
    all_gather x1, waiting for transfers between devices, per_device(): lax.all_gather(butterfly, 'dp', axis=2, tiled=True)  47.8 us
    psum x1, waiting for transfers between devices, per_device(): grad_low = lax.psum(low_back.astype(jnp.bfloat16), 'tensor')  42 us
    ppermute x4, waiting for transfers between devices, swapped(): return lax.ppermute(block, axis, route)  21.2 us
    all_gather x1, blocking collectives, per_device(): lax.all_gather(left_factor, 'dp', axis=0, tiled=True)  16.8 us
    reshape x2, local copies, waits for them, and re-layouts, per_device(): grad_wide = grad_pre.reshape(rows_here, blocks_here, group_ratio, BLK)  15.4 us
    convert_element_type x1, local copies, waits for them, and re-layouts, per_device(): grad_weight.astype(jnp.bfloat16)  15.2 us
    dot_general x1, matrix products, per_device(): jnp.einsum('tqro,qrkio->ktqi', grad_wide, weight_blocks, preferred_elemen...  12.8 us
  transfers between devices with their start and end apart: 11, of which 7 were waited for; matrix products, arithmetic and copies ran while one was open for 34% of the time, Pallas kernels for 0%

commit v1 on v0

--- a/solution.py
+++ b/solution.py
@@ -68,7 +68,9 @@
     )
     grad_weight = grad_weight.reshape(hidden_blocks, LOG + 1, BLK, BLK)
     low_back = jnp.einsum("th,rh->tr", grad_pre, right_full, preferred_element_type=jnp.float32)
-    grad_low = lax.psum(low_back.astype(jnp.bfloat16), "tensor")
+    own = low_back.astype(jnp.bfloat16)
+    pieces = lax.all_gather(own, "tensor", axis=0, tiled=False)
+    grad_low = pieces.sum(axis=0)
     grad_first = jnp.einsum("td,tr->dr", tokens, grad_low, preferred_element_type=jnp.float32)
     grad_second = jnp.einsum("tr,th->rh", low_rank, grad_pre, preferred_element_type=jnp.float32)
     returned = jnp.einsum(

time: 388 us -> 372 us (0.959)
  waiting for transfers between devices: 200 us -> 188 us
    psum x1 -> x0, waiting for transfers between devices: 42 us -> none  [per_device(): grad_low = lax.psum(low_back.astype(jnp.bfloat16), 'tensor')]
    all_gather x0 -> x1, waiting for transfers between devices: none -> 26 us  [per_device(): pieces = lax.all_gather(own, 'tensor', axis=0, tiled=False)]
    unnamed x22 -> x18, local copies, waits for them, and re-layouts: 12 us -> 12.1 us
where the time goes in v1:
time: 372 us; the launch traced here: 371 us
  waiting for transfers between devices  188 us (51%)
  local copies, waits for them, and re-layouts  81.6 us (22%)
  matrix products  56.1 us (15%)
  blocking collectives  16.8 us (5%)
  between operations  15.3 us (4%)
  other arithmetic  7.7 us (2%)
  starting transfers between devices  5.5 us (1%)
    reduce_scatter x1, waiting for transfers between devices, per_device(): lax.psum_scatter(grad_weight.astype(jnp.bfloat16), 'dp', scatter_dimensio...  80.8 us
    all_gather x1, waiting for transfers between devices, per_device(): lax.all_gather(butterfly, 'dp', axis=2, tiled=True)  47.8 us
    all_gather x1, waiting for transfers between devices, per_device(): pieces = lax.all_gather(own, 'tensor', axis=0, tiled=False)  26 us
    ppermute x4, waiting for transfers between devices, swapped(): return lax.ppermute(block, axis, route)  23.4 us
    all_gather x1, blocking collectives, per_device(): lax.all_gather(left_factor, 'dp', axis=0, tiled=True)  16.8 us
    reshape x2, local copies, waits for them, and re-layouts, per_device(): grad_wide = grad_pre.reshape(rows_here, blocks_here, group_ratio, BLK)  15.4 us
    convert_element_type x1, local copies, waits for them, and re-layouts, per_device(): grad_weight.astype(jnp.bfloat16)  15.1 us
    dot_general x1, matrix products, per_device(): jnp.einsum('tqro,qrkio->ktqi', grad_wide, weight_blocks, preferred_elemen...  12.7 us
  transfers between devices with their start and end apart: 11, of which 7 were waited for; matrix products, arithmetic and copies ran while one was open for 34% of the time, Pallas kernels for 0%

profile of v1, /device:TPU:0, one launch (start us, length us, event | category | flops | bytes accessed | tf_op | source)
XLA Modules:
  0.0 371.0 jit_solution(3722732126414042587)
XLA Ops:
  8.8 16.8 %all_gather.16 = bf16[1024,256]{1,0:T(8,128)(2,1)S(1)} all-gather(bf16[128,256]{1,0:T(8,128)(2,1)} %param.7), channel_id=1, replica_groups=mesh['dp'=8,'tensor'=4] {'dp'}, dimensions={0}, use_global_device_ids=true | all-gather | bytes 589824 | tf_op jit(solution)/shard_map/all_gather | solution.py:43
  26.4 2.4 convolution_convert_fusion.4
  35.5 1.6 reshape_reshape.7
  39.1 2.3 copy.42
  42.8 2.4 copy.41
  45.2 2.3 rev.16
  48.5 2.3 constant_dynamic-update-slice_fusion.1
  51.8 8.5 %collective-permute-done = bf16[512,4,256]{2,0,1:T(8,128)(2,1)} collective-permute-done((bf16[512,4,256]{2,0,1:T(8,128)(2,1)}, bf16[512,4,256]{2,0,1:T(8,128)(2,1)}, u32[]{:S(2)}, u32[]{:S(2)}) %collective-permute-start) | collective-permute-done | bytes 1048608 | tf_op jit(solution)/shard_map/ppermute | solution.py:19
  60.3 2.3 bitcast_dynamic-update-slice_fusion.1
  62.6 2.3 bitcast_dynamic-update-slice_fusion
  64.8 47.8 %all-gather.5.cloned.1.call-done = bf16[16,5,256,256]{3,2,1,0:T(8,128)(2,1)} async-done(((bf16[16,5,32,256]{3,2,1,0:T(8,128)(2,1)}), bf16[16,5,256,256]{3,2,1,0:T(8,128)(2,1)}) %all-gather.5.cloned.1.call-update) | async-done | bytes 10485776 | tf_op jit(solution)/shard_map/all_gather | solution.py:42
  112.6 12.0 %fusion.6 = f32[4,512,4,256,1]{1,3,4,2,0:T(8,128)} fusion(bf16[4,4,5,256,256]{4,3,2,1,0:T(8,128)(2,1)} %bitcast.95, bf16[5,512,4,256]{3,1,0,2:T(8,128)(2,1)} %bitcast_dynamic-update-slice_fusion), kind=kOutput, calls=%fused_computation.11 | convolution fusion | flops 5368709120 | bytes 24117248 | tf_op jit(solution)/shard_map/ktqi,qrkio->tqro/dot_general | solution.py:55
  124.6 9.0 %copy.48 = f32[512,4096]{1,0:T(8,128)} copy(f32[512,4096]{0,1:T(8,128)} %bitcast.89) | data formatting | bytes 16777216 | tf_op jit(solution)/shard_map/reshape | solution.py:58
  133.5 8.6 %all-gather.7.cloned.1.call-done = bf16[256,4096]{1,0:T(8,128)(2,1)} async-done(((bf16[32,4096]{1,0:T(8,128)(2,1)}), bf16[256,4096]{1,0:T(8,128)(2,1)}) %all-gather.7.cloned.1.call-update) | async-done | bytes 2097168 | tf_op jit(solution)/shard_map/all_gather | solution.py:44
  142.1 10.0 %fusion.4 = (bf16[512,4096]{1,0:T(8,128)(2,1)S(1)}, bf16[512,4096]{1,0:T(8,128)(2,1)}) fusion(bf16[512,4096]{1,0:T(8,128)(2,1)} %param.9, f32[512,4096]{1,0:T(8,128)} %copy.48, bf16[512,256]{1,0:T(8,128)(2,1)} %all-reduce.2.cloned.1.call-done, bf16[256,4096]{1,0:T(8,128)(2,1)} %all-gather.7.cloned.1.call-done), kind=kOutput, calls=%fused_computation.5 | convolution fusion | flops 1103101952 | bytes 23330816 | tf_op jit(solution)/shard_map/dot_general | solution.py:61
  152.1 2.1 copy-done.1
  154.2 2.0 convolution_convert_fusion.3
  156.3 26.0 %all-gather.9.cloned.1.call-done = bf16[2048,256]{1,0:T(8,128)(2,1)} async-done(((bf16[512,256]{1,0:T(8,128)(2,1)}), bf16[2048,256]{1,0:T(8,128)(2,1)}) %all-gather.9.cloned.1.call-update) | async-done | bytes 1048592 | tf_op jit(solution)/shard_map/all_gather | solution.py:72
  185.5 4.8 %convolution_convert_fusion.1 = bf16[256,4096]{1,0:T(8,128)(2,1)} fusion(bf16[512,256]{1,0:T(8,128)(2,1)S(1)} %copy-done.4, bf16[512,4096]{1,0:T(8,128)(2,1)} %copy-done.1), kind=kOutput, calls=%fused_computation.13 | convolution fusion | flops 1074790400 | bytes 6553600 | tf_op jit(solution)/shard_map/tr,th->rh/dot_general | solution.py:75
  190.4 7.9 %reshape.38 = bf16[512,4,4,256]{3,2,1,0:T(4,128)(2,1)} reshape(bf16[512,4096]{1,0:T(8,128)(2,1)} %copy-done.1) | data formatting | bytes 8388608 | tf_op jit(solution)/shard_map/reshape | solution.py:65
  198.3 7.5 %copy.62 = bf16[512,4,4,256,1]{0,3,4,2,1:T(8,128)(2,1)} copy(bf16[512,4,4,256,1]{3,2,1,0,4:T(4,128)(2,1)} %bitcast.84) | data formatting | bytes 8388608 | tf_op jit(solution)/shard_map/reshape | solution.py:65
  205.8 11.3 %convolution_convert_fusion = bf16[4,4,256,5,256]{4,2,3,1,0:T(8,128)(2,1)} fusion(bf16[512,4,4,256,1]{0,3,4,2,1:T(8,128)(2,1)} %copy.62, bf16[5,512,4,256]{3,1,0,2:T(8,128)(2,1)} %bitcast_dynamic-update-slice_fusion), kind=kOutput, calls=%fused_computation.9 | convolution fusion | flops 5373952000 | bytes 19922944 | tf_op jit(solution)/shard_map/ktqi,tqro->qrkio/dot_general | solution.py:66
  217.1 15.1 %copy.55 = bf16[16,5,256,256]{3,2,1,0:T(8,128)(2,1)} copy(bf16[16,5,256,256]{2,3,1,0:T(8,128)(2,1)} %bitcast.85) | data formatting | bytes 20971520 | tf_op jit(solution)/shard_map/convert_element_type | solution.py:94
  232.3 12.7 %fusion.14 = (bf16[5,512,4,256]{1,3,0,2:T(8,128)(2,1)}, f32[5,512,4,256]{1,3,0,2:T(8,128)}) fusion(bf16[512,4,4,256,1]{0,3,4,2,1:T(8,128)(2,1)} %copy.62, bf16[4,4,5,256,256]{4,3,2,1,0:T(8,128)(2,1)} %bitcast.96), kind=kOutput, calls=%fused_computation.33 | convolution fusion | flops 5371330560 | bytes 30408704 | tf_op jit(solution)/shard_map/tqro,qrkio->ktqi/dot_general | solution.py:76
  245.0 3.0 slice_bitcast_fusion.2
  250.1 4.6 %fusion.13 = (f32[1,512,4,256]{1,3,0,2:T(8,128)}, f32[1,512,4,256]{1,3,0,2:T(8,128)}) fusion(f32[5,512,4,256]{1,3,0,2:T(8,128)} %get-tuple-element.27), kind=kLoop, calls=%fused_computation.32 | loop fusion | bytes 8388608 | tf_op jit(solution)/shard_map/slice | solution.py:81
  254.7 1.8 rev.18
  256.5 3.1 rev.19
  259.6 13.7 %collective-permute-done.2 = bf16[512,4,256]{0,2,1:T(8,128)(2,1)} collective-permute-done((bf16[512,4,256]{0,2,1:T(8,128)(2,1)}, bf16[512,4,256]{0,2,1:T(8,128)(2,1)}, u32[]{:S(2)}, u32[]{:S(2)}) %collective-permute-start.2) | collective-permute-done | bytes 1048608 | tf_op jit(solution)/shard_map/ppermute | solution.py:19
  274.4 5.0 %fusion.11 = f32[512,4,256]{0,2,1:T(8,128)} fusion(f32[5,512,4,256]{1,3,0,2:T(8,128)} %get-tuple-element.27, f32[512,1,2,2,256]{0,4,3,2,1:T(8,128)} %rev.19, f32[512,2,2,1,256]{0,4,2,1,3:T(8,128)S(1)} %rev.18, bf16[512,4,256]{0,2,1:T(8,128)(2,1)} %collective-permute-done.3, bf16[512,4,256]{0,2,1:T(8,128)(2,1)} %collective-permute-done.2), kind=kLoop, calls=%fused_computation.19 | loop fusion | flops 3145728 | bytes 10485760 | tf_op jit(solution)/shard_map/add | solution.py:85
  279.4 1.9 copy.53
  283.1 80.8 %reduce-scatter.6.cloned.1.call-done = bf16[16,5,32,256]{3,2,1,0:T(8,128)(2,1)} async-done(((bf16[16,5,256,256]{3,2,1,0:T(8,128)(2,1)}), bf16[16,5,32,256]{3,2,1,0:T(8,128)(2,1)}) %reduce-scatter.6.cloned.1.call-update) | async-done | bytes 1310736 | tf_op jit(solution)/shard_map/reduce_scatter | solution.py:93
  (46 shorter events, 22.0 us)
Async XLA Ops:
  8.0 27.5 %copy-start = (bf16[512,1024]{1,0:T(8,128)(2,1)S(1)}, bf16[512,1024]{1,0:T(8,128)(2,1)}, u32[]{:S(2)}) copy-start(bf16[512,1024]{1,0:T(8,128)(2,1)} %param.5) | copy-start | bytes 3145732
  8.0 104.6 %all-gather.5.cloned.1.call-start = ((), (), s32[]{:S(2)}) async-start(), calls=%async_computation.3 | async-start | bytes 11796480 | tf_op jit(solution)/shard_map/all_gather | solution.py:42
  8.7 124.8 %all-reduce.2.cloned.1.call-start = ((), (), s32[]{:S(2)}) async-start(), calls=%async_computation.4 | async-start | bytes 524288 | tf_op jit(solution)/shard_map/psum | solution.py:60
  25.6 0.8 copy-start.2
  28.8 113.3 %all-gather.7.cloned.1.call-start = ((), (), s32[]{:S(2)}) async-start(), calls=%async_computation.5 | async-start | bytes 2359296 | tf_op jit(solution)/shard_map/all_gather | solution.py:44
  29.6 152.7 %all-gather.9.cloned.1.call-start = ((), (), s32[]{:S(2)}) async-start(), calls=%async_computation.8 | async-start | bytes 1310720 | tf_op jit(solution)/shard_map/all_gather | solution.py:72
  32.5 27.8 %collective-permute-start = (bf16[512,4,256]{2,0,1:T(8,128)(2,1)}, bf16[512,4,256]{2,0,1:T(8,128)(2,1)}, u32[]{:S(2)}, u32[]{:S(2)}) collective-permute-start(bf16[512,4,256]{2,0,1:T(8,128)(2,1)} %copy.44), channel_id=1, source_target_pairs={{0,1},{1,0},{2,3},{3,2},{4,5},{5,4},{6,7},{7,6},{8,9},{9,8},{10,11... | collective-permute-start | bytes 3145736 | tf_op jit(solution)/shard_map/ppermute | solution.py:19
  34.0 28.6 %collective-permute-start.1 = (bf16[512,4,256]{2,0,1:T(8,128)(2,1)}, bf16[512,4,256]{2,0,1:T(8,128)(2,1)}, u32[]{:S(2)}, u32[]{:S(2)}) collective-permute-start(bf16[512,4,256]{2,0,1:T(8,128)(2,1)} %copy.44), channel_id=1, source_target_pairs={{0,2},{2,0},{1,3},{3,1},{4,6},{6,4},{5,7},{7,5},{8,10},{10,8},{9,1... | collective-permute-start | bytes 3145736 | tf_op jit(solution)/shard_map/ppermute | solution.py:19
  142.1 12.1 %copy-start.5 = (bf16[256,4096]{1,0:T(8,128)(2,1)S(1)}, bf16[256,4096]{1,0:T(8,128)(2,1)}, u32[]{:S(2)}) copy-start(bf16[256,4096]{1,0:T(8,128)(2,1)} %all-gather.7.cloned.1.call-done) | copy-start | bytes 6291460
  152.1 2.1 copy-start.1
  154.2 31.3 %copy-start.4 = (bf16[512,256]{1,0:T(8,128)(2,1)S(1)}, bf16[512,256]{1,0:T(8,128)(2,1)}, u32[]{:S(2)}) copy-start(bf16[512,256]{1,0:T(8,128)(2,1)} %all-reduce.2.cloned.1.call-done) | copy-start | bytes 786436
  156.2 126.9 %reduce-scatter.10.cloned.1.call-start = ((), (), s32[]{:S(2)}) async-start(), calls=%async_computation.9 | async-start | bytes 589824
  185.3 97.8 %reduce-scatter.8.cloned.1.call-start = ((), (), s32[]{:S(2)}) async-start(), calls=%async_computation.7 | async-start | bytes 2359296 | tf_op jit(solution)/shard_map/reduce_scatter | solution.py:99
  190.3 173.5 %reduce-scatter.6.cloned.1.call-start = ((), (), s32[]{:S(2)}) async-start(), calls=%async_computation.6 | async-start | bytes 11796480 | tf_op jit(solution)/shard_map/reduce_scatter | solution.py:93
  248.0 25.2 %collective-permute-start.2 = (bf16[512,4,256]{0,2,1:T(8,128)(2,1)}, bf16[512,4,256]{0,2,1:T(8,128)(2,1)}, u32[]{:S(2)}, u32[]{:S(2)}) collective-permute-start(bf16[512,4,256]{0,2,1:T(8,128)(2,1)} %get-tuple-element.24), channel_id=1, source_target_pairs={{0,1},{1,0},{2,3},{3,2},{4,5},{5,4},{6,7},{7,6},{8,9},{9,8},{10,11... | collective-permute-start | bytes 3145736 | tf_op jit(solution)/shard_map/ppermute | solution.py:19
  249.5 24.9 %collective-permute-start.3 = (bf16[512,4,256]{0,2,1:T(8,128)(2,1)}, bf16[512,4,256]{0,2,1:T(8,128)(2,1)}, u32[]{:S(2)}, u32[]{:S(2)}) collective-permute-start(bf16[512,4,256]{0,2,1:T(8,128)(2,1)} %get-tuple-element.25), channel_id=1, source_target_pairs={{0,2},{2,0},{1,3},{3,1},{4,6},{6,4},{5,7},{7,5},{8,10},{10,8},{9,1... | collective-permute-start | bytes 3145736 | tf_op jit(solution)/shard_map/ppermute | solution.py:19
  259.6 21.8 %copy-start.3 = (bf16[1024,256]{1,0:T(8,128)(2,1)S(1)}, bf16[1024,256]{1,0:T(8,128)(2,1)}, u32[]{:S(2)}) copy-start(bf16[1024,256]{1,0:T(8,128)(2,1)} %copy-done.2) | copy-start | bytes 1572868
Sparse Core Ops, SparseCore 0:
  10.4 102.0 all-gather.4
  114.3 27.8 all-gather.6
  185.4 30.9 reduce-scatter.9
  219.1 33.9 reduce-scatter.7
  255.9 107.9 reduce-scatter.5
Sparse Core Ops, SparseCore 1:
  28.9 46.1 all-reduce.1
  156.3 25.9 all-gather.8
